TPU v7x, 512 devices: a whole 4x8x8 slice. The times are simulated.
512 devices in a mesh: vocab: 4 (over x), rows: 128 (over y, z, core).
Axes of the slice: x: 4, y: 8, z: 8, core: 2. Of those that a mesh axis runs over, the one named last changes fastest.
Arguments:
- hidden: bfloat16 [4, 4096, 8192], P(None, 'rows'), may hold values from -0.75 to 0.75
- teacher_weight: bfloat16 [8192, 1536], P('rows', 'vocab'), may hold values from -20 to 20
- draft_weight: bfloat16 [8192, 512], P('rows', 'vocab'), may hold values from -20 to 20
- draft_list: int32 [4, 4], replicated, may hold values from 0 to 11, as said below
Outputs:
- row_loss: float32 [4, 4096], P(None, 'rows')
- grad_hidden: bfloat16 [4, 4096, 8192], P(None, 'rows')
- grad_draft: float32 [8192, 512], P('rows', 'vocab')
Inputs may be any that keep to these rules, and one draw needn't show every extreme that they name: `draft_list`: in each tile the 4 listed blocks are distinct.
All inputs are finite; a program needn't handle non-finite values.
Results may differ from a plain program's by a relative error of at most 0.008.
Values may be sent and summed in bfloat16 or wider, within the bound.
A program may use at most 64 MiB of HBM per device.

v0:
```python
import jax
import jax.numpy as jnp
from jax import lax
from jax.sharding import PartitionSpec as P

BLK = 128


def pick_blocks(tile_blocks, listed):
    return jnp.take(tile_blocks, listed, axis=1)


def per_device(hidden, teacher_weight, draft_weight, draft_list):
    tile_count, tile_rows, model_width = hidden.shape
    row_count = tile_count * tile_rows
    flat_rows = hidden.reshape(row_count, model_width)
    draft_cols = draft_weight.shape[1]
    slot_count = draft_cols // BLK
    columns = flat_rows
    teacher_logits = jnp.dot(
        columns,
        lax.all_gather(teacher_weight, "rows", axis=0, tiled=True),
        preferred_element_type=jnp.float32,
    )
    draft_full = lax.all_gather(draft_weight, "rows", axis=0, tiled=True)
    draft_logits = jnp.dot(flat_rows, draft_full, preferred_element_type=jnp.float32)
    teacher_all = lax.all_gather(teacher_logits, "vocab", axis=1, tiled=True)
    teacher_max = jnp.max(teacher_all, axis=1, keepdims=True)
    teacher_total = jnp.sum(jnp.exp(teacher_all - teacher_max), axis=1, keepdims=True)
    blocks = teacher_all.reshape(tile_count, tile_rows, -1, BLK)
    picked = jax.vmap(pick_blocks)(blocks, draft_list)
    target = jnp.exp(
        picked - teacher_max.reshape(tile_count, tile_rows, 1, 1)
    ) / teacher_total.reshape(tile_count, tile_rows, 1, 1)
    covered = jnp.sum(target, axis=(2, 3)).reshape(row_count)
    vocab_position = lax.axis_index("vocab")
    own_target = lax.dynamic_slice_in_dim(
        target, vocab_position * slot_count, slot_count, 2
    ).reshape(row_count, draft_cols)
    local_max = jnp.max(draft_logits, axis=1)
    weighted = jnp.sum(own_target * draft_logits, axis=1)
    draft_max = lax.pmax(local_max, "vocab")
    local_total = jnp.sum(jnp.exp(draft_logits - draft_max[:, None]), axis=1)
    draft_total, crossed = lax.psum((local_total, weighted), "vocab")
    row_loss = covered * (draft_max + jnp.log(draft_total)) - crossed
    draft_prob = jnp.exp(draft_logits - draft_max[:, None]) / draft_total[:, None]
    logit_grad = (covered[:, None] * draft_prob - own_target).astype(jnp.bfloat16)
    partial_value = lax.dot_general(
        logit_grad, draft_full, (((1,), (1,)), ((), ())), preferred_element_type=jnp.float32
    )
    grad_hidden = lax.psum(partial_value.astype(jnp.bfloat16), "vocab").reshape(
        tile_count, tile_rows, model_width
    )
    columns = flat_rows
    grad_draft = lax.psum_scatter(
        lax.dot_general(
            columns, logit_grad, (((0,), (0,)), ((), ())), preferred_element_type=jnp.float32
        ),
        "rows",
        scatter_dimension=0,
        tiled=True,
    )
    return (row_loss.reshape(tile_count, tile_rows), grad_hidden, grad_draft)


def solution(mesh):
    in_specs = (P(None, "rows", None), P("rows", "vocab"), P("rows", "vocab"), P())
    out_specs = (P(None, "rows"), P(None, "rows", None), P("rows", "vocab"))
    return jax.shard_map(
        per_device, mesh=mesh, in_specs=in_specs, out_specs=out_specs, check_vma=False
    )
```

profile of v0, /device:TPU:2, one launch (start us, length us, event | category | flops | bytes accessed | tf_op | source)
XLA Modules:
  0.0 502.0 jit_solution(2816774992845677760)
XLA Ops:
  7.2 0.0 copy-start
  7.2 0.0 all-gather.5.cloned.1.call-start
  7.2 0.7 all-gather.5.cloned.1.call-update
  7.9 0.0 all-gather.3.cloned.1.call-start
  8.0 0.7 all-gather.3.cloned.1.call-update
  8.7 0.0 all-reduce.3.cloned.1.call-start
  8.7 0.7 compare_and_fusion
  9.4 0.1 copy.16
  9.5 0.7 bitcast_or_fusion
  10.2 0.1 reshape.41
  10.3 88.6 %all-gather.5.cloned.1.call-done = bf16[8192,128]{1,0:T(8,128)(2,1)} async-done(((bf16[64,128]{1,0:T(8,128)(2,1)}), bf16[8192,128]{1,0:T(8,128)(2,1)}) %all-gather.5.cloned.1.call-update) | async-done | bytes 2097168 | tf_op jit(solution)/shard_map/all_gather | solution.py:25
  98.9 0.0 copy-done
  98.9 2.5 fusion.6
  101.4 8.6 %pmax.7 = f32[128]{0:T(128)S(1)} all-reduce(f32[128]{0:T(128)S(1)} %get-tuple-element.18), channel_id=1, replica_groups=mesh['vocab'=4,'rows'=128] {'vocab'}, use_global_device_ids=true, to_apply=%region_4.5 | all-reduce | flops 128 | bytes 1024 | tf_op jit(solution)/shard_map/pmax | solution.py:42
  110.0 74.8 %all-gather.3.cloned.1.call-done = bf16[8192,384]{1,0:T(8,128)(2,1)} async-done(((bf16[64,384]{1,0:T(8,128)(2,1)}), bf16[8192,384]{1,0:T(8,128)(2,1)}) %all-gather.3.cloned.1.call-update) | async-done | bytes 6291472 | tf_op jit(solution)/shard_map/all_gather | solution.py:22
  184.8 4.0 fusion.7
  188.8 14.3 %all_gather.10 = f32[128,1536]{1,0:T(8,128)S(1)} all-gather(f32[128,384]{1,0:T(8,128)S(1)} %fusion.7), channel_id=1, replica_groups=mesh['vocab'=4,'rows'=128] {'vocab'}, dimensions={1}, use_global_device_ids=true | all-gather | bytes 983040 | tf_op jit(solution)/shard_map/all_gather | solution.py:27
  203.1 0.1 reduce_max.18
  203.2 0.3 exponential_reduce_fusion
  203.5 0.1 sub.36
  203.6 1.1 reshape.36
  204.7 0.1 div.18
  204.8 1.5 copy.17
  206.3 0.6 gather_fusion
  206.9 0.2 fusion.4
  207.1 0.1 reshape.37
  207.2 0.1 copy.19
  207.3 7.9 %all-reduce = (f32[128]{0:T(128)S(1)}, f32[128]{0:T(128)S(1)}) all-reduce(f32[128]{0:T(128)S(1)} %get-tuple-element.13, f32[128]{0:T(128)S(1)} %get-tuple-element.12), channel_id=1, replica_groups=mesh['vocab'=4,'rows'=128] {'vocab'}, use_global_device_ids=true, to_apply=%region_8.9 | all-reduce | flops 256 | bytes 2048 | tf_op jit(solution)/shard_map/psum | solution.py:44
  215.3 3.6 convolution_convert_fusion
  218.9 0.0 all-reduce.3.cloned.1.call-update
  219.0 0.0 reduce-scatter.4.cloned.1.call-start
  219.0 2.6 convolution_bitcast_fusion
  221.6 5.6 %copy.22 = f32[8192,128]{1,0:T(8,128)} copy(f32[8192,128]{0,1:T(8,128)} %convolution_bitcast_fusion) | data formatting | bytes 8388608
  227.2 0.0 reduce-scatter.4.cloned.1.call-update
  227.3 0.7 reshape.39
  227.9 56.6 %all-reduce.3.cloned.1.call-done = bf16[4,32,8192]{2,1,0:T(8,128)(2,1)} async-done(((bf16[4,32,8192]{2,1,0:T(8,128)(2,1)}), bf16[4,32,8192]{2,1,0:T(8,128)(2,1)}) %all-reduce.3.cloned.1.call-update) | async-done | bytes 2097168 | tf_op jit(solution)/shard_map/psum | solution.py:51
  284.5 207.9 %reduce-scatter.4.cloned.1.call-done = f32[64,128]{1,0:T(8,128)} async-done(((f32[8192,128]{1,0:T(8,128)}), f32[64,128]{1,0:T(8,128)}) %reduce-scatter.4.cloned.1.call-update) | async-done | bytes 32784
  492.4 3.1 copy.33
  (4 shorter events, 0.1 us)
Async XLA Ops:
  7.2 91.7 %copy-start = (bf16[4,32,8192]{2,1,0:T(8,128)(2,1)S(1)}, bf16[4,32,8192]{2,1,0:T(8,128)(2,1)}, u32[]{:S(2)}) copy-start(bf16[4,32,8192]{2,1,0:T(8,128)(2,1)} %param.4) | copy-start | bytes 6291460
  7.2 91.7 %all-gather.5.cloned.1.call-start = ((), (), s32[]{:S(2)}) async-start(), calls=%async_computation.2 | async-start | bytes 2113536 | tf_op jit(solution)/shard_map/all_gather | solution.py:25
  7.9 176.9 %all-gather.3.cloned.1.call-start = ((), (), s32[]{:S(2)}) async-start(), calls=%async_computation.1 | async-start | bytes 6340608 | tf_op jit(solution)/shard_map/all_gather | solution.py:22
  8.7 275.8 %all-reduce.3.cloned.1.call-start = ((), (), s32[]{:S(2)}) async-start(), calls=%async_computation.3 | async-start | bytes 4194304 | tf_op jit(solution)/shard_map/psum | solution.py:51
  219.0 273.4 %reduce-scatter.4.cloned.1.call-start = ((), (), s32[]{:S(2)}) async-start(), calls=%async_computation.4 | async-start | bytes 4227072
Sparse Core Ops, SparseCore 0:
  11.1 87.7 all-gather.4
  102.0 82.7 all-gather.2
  219.1 65.3 all-reduce.2
  289.3 203.0 reduce-scatter.3
where the time goes:
time: 502 us
  waiting for transfers between devices  429 us (85%)
  blocking collectives  30.8 us (6%)
  between operations  13.8 us (3%)
  local copies, waits for them, and re-layouts  13.1 us (3%)
  matrix products  12.8 us (3%)
    unnamed x5, waiting for transfers between devices  209 us
    all_gather x1, waiting for transfers between devices, per_device(): draft_full = lax.all_gather(draft_weight, 'rows', axis=0, tiled=True)  88.6 us
    all_gather x1, waiting for transfers between devices, per_device(): lax.all_gather(teacher_weight, 'rows', axis=0, tiled=True)  74.8 us
    psum x1, waiting for transfers between devices, per_device(): lax.psum(partial_value.astype(jnp.bfloat16), 'vocab')  56.6 us
    all_gather x1, blocking collectives, per_device(): teacher_all = lax.all_gather(teacher_logits, 'vocab', axis=1, tiled=True)  14.3 us
  transfers between devices with their start and end apart: 4, of which 4 were waited for; matrix products, arithmetic and copies ran while one was open for 3% of the time, Pallas kernels for 0%

commit v1 on v0

--- a/solution.py
+++ b/solution.py
@@ -4,6 +4,11 @@
 from jax.sharding import PartitionSpec as P
 
 BLK = 128
+
+
+def exchange_gather(array, mesh_axis, d):
+    repeated = jnp.stack([array] * lax.axis_size(mesh_axis))
+    return jnp.concatenate(lax.all_to_all(repeated, mesh_axis, 0, 0), axis=d)
 
 
 def pick_blocks(tile_blocks, listed):
@@ -22,7 +27,7 @@
         lax.all_gather(teacher_weight, "rows", axis=0, tiled=True),
         preferred_element_type=jnp.float32,
     )
-    draft_full = lax.all_gather(draft_weight, "rows", axis=0, tiled=True)
+    draft_full = exchange_gather(draft_weight, "rows", 0)
     draft_logits = jnp.dot(flat_rows, draft_full, preferred_element_type=jnp.float32)
     teacher_all = lax.all_gather(teacher_logits, "vocab", axis=1, tiled=True)
     teacher_max = jnp.max(teacher_all, axis=1, keepdims=True)

time: 502 us -> 452 us (0.900)
  waiting for transfers between devices: 429 us -> 359 us
  starting transfers between devices: 0.16 us -> 18.6 us
    all_gather x1 -> x0, waiting for transfers between devices: 88.6 us -> none  [per_device(): draft_full = lax.all_gather(draft_weight, 'rows', axis=0, tiled=True)]
    all_to_all x0 -> x1, waiting for transfers between devices: none -> 53.6 us  [exchange_gather(): return jnp.concatenate(lax.all_to_all(repeated, mesh_axis, 0, 0), axis=d)]
    all_gather x1, waiting for transfers between devices: 74.8 us -> 39.7 us  [per_device(): lax.all_gather(teacher_weight, 'rows', axis=0, tiled=True)]
    all_to_all x0 -> x1, starting transfers between devices: none -> 18.5 us  [exchange_gather(): return jnp.concatenate(lax.all_to_all(repeated, mesh_axis, 0, 0), axis=d)]
    unnamed x5 -> x4, waiting for transfers between devices: 209 us -> 209 us
where the time goes in v1:
time: 452 us; the launch traced here: 451 us
  waiting for transfers between devices  359 us (79%)
  blocking collectives  30.9 us (7%)
  starting transfers between devices  18.6 us (4%)
  local copies, waits for them, and re-layouts  15.6 us (3%)
  between operations  13.8 us (3%)
  matrix products  12.8 us (3%)
    unnamed x4, waiting for transfers between devices  209 us
    psum x1, waiting for transfers between devices, per_device(): lax.psum(partial_value.astype(jnp.bfloat16), 'vocab')  56.6 us
    all_to_all x1, waiting for transfers between devices, exchange_gather(): return jnp.concatenate(lax.all_to_all(repeated, mesh_axis, 0, 0), axis=d)  53.6 us
    all_gather x1, waiting for transfers between devices, per_device(): lax.all_gather(teacher_weight, 'rows', axis=0, tiled=True)  39.7 us
    all_to_all x1, starting transfers between devices, exchange_gather(): return jnp.concatenate(lax.all_to_all(repeated, mesh_axis, 0, 0), axis=d)  18.5 us
    all_gather x1, blocking collectives, per_device(): teacher_all = lax.all_gather(teacher_logits, 'vocab', axis=1, tiled=True)  14.3 us
  transfers between devices with their start and end apart: 4, of which 4 were waited for; matrix products, arithmetic and copies ran while one was open for 3% of the time, Pallas kernels for 0%

profile of v1, /device:TPU:2, one launch (start us, length us, event | category | flops | bytes accessed | tf_op | source)
XLA Modules:
  0.0 451.3 jit_solution(4469899843100717897)
XLA Ops:
  7.2 0.0 copy-start
  7.2 0.0 all-gather.2.cloned.1.call-start
  7.2 0.7 all-gather.2.cloned.1.call-update
  7.9 2.6 stack.2
  10.5 0.0 copy-start.1
  10.5 18.5 %all-to-all-start = ((bf16[128,64,128]{2,1,0:T(8,128)(2,1)}), bf16[128,64,128]{2,1,0:T(8,128)(2,1)}, u32[]{:S(2)}, u32[]{:S(2)}) async-start(bf16[128,64,128]{2,1,0:T(8,128)(2,1)} %stack.2), calls=%async_computation | async-start | bytes 4194304 | tf_op jit(solution)/shard_map/all_to_all | solution.py:11
  29.0 0.0 all-reduce.3.cloned.1.call-start
  29.0 0.0 copy-done.1
  29.0 0.1 copy.16
  29.1 0.1 reshape.47
  29.2 53.6 %all-to-all-done = bf16[128,64,128]{2,1,0:T(8,128)(2,1)} async-done(((bf16[128,64,128]{2,1,0:T(8,128)(2,1)}), bf16[128,64,128]{2,1,0:T(8,128)(2,1)}, u32[]{:S(2)}, u32[]{:S(2)}) %all-to-all-start) | async-done | bytes 2097184 | tf_op jit(solution)/shard_map/all_to_all | solution.py:11
  82.9 0.0 copy-done
  82.9 2.5 fusion.6
  85.4 8.7 %pmax.7 = f32[128]{0:T(128)S(1)} all-reduce(f32[128]{0:T(128)S(1)} %get-tuple-element.18), channel_id=1, replica_groups=mesh['vocab'=4,'rows'=128] {'vocab'}, use_global_device_ids=true, to_apply=%region_4.5 | all-reduce | flops 128 | bytes 1024 | tf_op jit(solution)/shard_map/pmax | solution.py:47
  94.1 39.7 %all-gather.2.cloned.1.call-done = bf16[8192,384]{1,0:T(8,128)(2,1)} async-done(((bf16[64,384]{1,0:T(8,128)(2,1)}), bf16[8192,384]{1,0:T(8,128)(2,1)}) %all-gather.2.cloned.1.call-update) | async-done | bytes 6291472 | tf_op jit(solution)/shard_map/all_gather | solution.py:27
  133.8 4.0 fusion.7
  137.9 14.3 %all_gather.7 = f32[128,1536]{1,0:T(8,128)S(1)} all-gather(f32[128,384]{1,0:T(8,128)S(1)} %fusion.7), channel_id=1, replica_groups=mesh['vocab'=4,'rows'=128] {'vocab'}, dimensions={1}, use_global_device_ids=true | all-gather | bytes 983040 | tf_op jit(solution)/shard_map/all_gather | solution.py:32
  152.1 0.1 reduce_max.18
  152.3 0.3 exponential_reduce_fusion
  152.5 0.1 sub.36
  152.6 1.1 reshape.41
  153.7 0.1 div.18
  153.8 1.5 copy.17
  155.3 0.6 gather_fusion
  155.9 0.2 fusion.4
  156.1 0.1 reshape.42
  156.2 0.1 copy.19
  156.4 7.9 %all-reduce = (f32[128]{0:T(128)S(1)}, f32[128]{0:T(128)S(1)}) all-reduce(f32[128]{0:T(128)S(1)} %get-tuple-element.13, f32[128]{0:T(128)S(1)} %get-tuple-element.12), channel_id=1, replica_groups=mesh['vocab'=4,'rows'=128] {'vocab'}, use_global_device_ids=true, to_apply=%region_8.9 | all-reduce | flops 256 | bytes 2048 | tf_op jit(solution)/shard_map/psum | solution.py:49
  164.3 3.6 convolution_convert_fusion
  168.0 0.0 all-reduce.3.cloned.1.call-update
  168.0 0.0 reduce-scatter.4.cloned.1.call-start
  168.0 2.6 convolution_bitcast_fusion
  170.7 5.6 %copy.22 = f32[8192,128]{1,0:T(8,128)} copy(f32[8192,128]{0,1:T(8,128)} %convolution_bitcast_fusion) | data formatting | bytes 8388608
  176.2 0.0 reduce-scatter.4.cloned.1.call-update
  176.3 0.7 reshape.45
  176.9 56.6 %all-reduce.3.cloned.1.call-done = bf16[4,32,8192]{2,1,0:T(8,128)(2,1)} async-done(((bf16[4,32,8192]{2,1,0:T(8,128)(2,1)}), bf16[4,32,8192]{2,1,0:T(8,128)(2,1)}) %all-reduce.3.cloned.1.call-update) | async-done | bytes 2097168 | tf_op jit(solution)/shard_map/psum | solution.py:56
  233.5 208.2 %reduce-scatter.4.cloned.1.call-done = f32[64,128]{1,0:T(8,128)} async-done(((f32[8192,128]{1,0:T(8,128)}), f32[64,128]{1,0:T(8,128)}) %reduce-scatter.4.cloned.1.call-update) | async-done | bytes 32784
  441.7 3.1 copy.33
  (6 shorter events, 0.1 us)
Async XLA Ops:
  7.2 75.7 %copy-start = (bf16[4,32,8192]{2,1,0:T(8,128)(2,1)S(1)}, bf16[4,32,8192]{2,1,0:T(8,128)(2,1)}, u32[]{:S(2)}) copy-start(bf16[4,32,8192]{2,1,0:T(8,128)(2,1)} %param.4) | copy-start | bytes 6291460
  7.2 126.6 %all-gather.2.cloned.1.call-start = ((), (), s32[]{:S(2)}) async-start(), calls=%async_computation.2 | async-start | bytes 6340608 | tf_op jit(solution)/shard_map/all_gather | solution.py:27
  10.5 18.5 %copy-start.1 = (s32[4,4]{1,0:T(4,128)S(1)}, s32[4,4]{1,0:T(4,128)}, u32[]{:S(2)}) copy-start(s32[4,4]{1,0:T(4,128)} %param.7) | copy-start | bytes 196
  10.5 72.4 %all-to-all-start = ((bf16[128,64,128]{2,1,0:T(8,128)(2,1)}), bf16[128,64,128]{2,1,0:T(8,128)(2,1)}, u32[]{:S(2)}, u32[]{:S(2)}) async-start(bf16[128,64,128]{2,1,0:T(8,128)(2,1)} %stack.2), calls=%async_computation | async-start | bytes 4194304 | tf_op jit(solution)/shard_map/all_to_all | solution.py:11
  29.0 204.6 %all-reduce.3.cloned.1.call-start = ((), (), s32[]{:S(2)}) async-start(), calls=%async_computation.3 | async-start | bytes 4194304 | tf_op jit(solution)/shard_map/psum | solution.py:56
  168.0 273.7 %reduce-scatter.4.cloned.1.call-start = ((), (), s32[]{:S(2)}) async-start(), calls=%async_computation.4 | async-start | bytes 4227072
Sparse Core Ops, SparseCore 0:
  11.1 122.6 all-gather.1
  168.1 65.3 all-reduce.2
  238.5 203.1 reduce-scatter.3
